TPU v7x, 512 devices: a whole 4x8x8 slice. The times are simulated.
512 devices in a mesh: seq: 64 (over y, x, core), head: 8 (over z).
Axes of the slice: x: 4, y: 8, z: 8, core: 2. Of those that a mesh axis runs over, the one named last changes fastest.
Arguments:
- hidden_states: bfloat16 [49152, 8192], P('seq', 'head'), may hold values from -6 to 6
- k_weight: bfloat16 [8192, 1024], P('head', 'seq'), may hold values from -0.0625 to 0.0625
- v_weight: bfloat16 [8192, 1024], P('head', 'seq'), may hold values from -0.0625 to 0.0625
- assignments: int32 [8, 49152], P('head', 'seq'), may hold values from 0 to 1023
- old_centroids: float32 [8, 1024, 128], P('head'), may hold values from -6 to 6
Outputs:
- key_cache: bfloat16 [49152, 1024], P('seq', 'head')
- value_cache: bfloat16 [49152, 1024], P('seq', 'head')
- new_centroids: float32 [8, 1024, 128], P('head', 'seq')
- distances: bfloat16 [8, 49152, 1024], P('head', 'seq')
All inputs are finite; a program needn't handle non-finite values.
Results may differ from a plain program's by a relative error of at most 0.017.
Values may be sent and summed in bfloat16 or wider, within the bound.
A program may use at most 64 MiB of HBM per device.

v0:
```python
import jax
import jax.numpy as jnp
from jax import lax
from jax.sharding import PartitionSpec as P


def shards(hidden_states, k_weight, v_weight, assignments, old_centroids):
    tok_rows = hidden_states.shape[0]
    heads_local = old_centroids.shape[0]
    clusters = old_centroids.shape[1]
    head_size = old_centroids.shape[2]
    stacked = jnp.stack((k_weight, v_weight), axis=1)
    partial_terms = jnp.einsum(
        "td,dkc->tkc",
        hidden_states,
        lax.all_gather(stacked, "seq", axis=2, tiled=True),
        preferred_element_type=jnp.float32,
    )
    summed = lax.psum_scatter(
        partial_terms.astype(jnp.bfloat16), "head", scatter_dimension=2, tiled=True
    ).astype(jnp.float32)
    key_cache = summed[:, 0].astype(jnp.bfloat16)
    value_cache = summed[:, 1].astype(jnp.bfloat16)
    key_heads = key_cache.reshape(tok_rows, heads_local, head_size)
    onehot = (
        assignments[:, :, None] == jnp.arange(clusters, dtype=jnp.int32)[None, None, :]
    ).astype(jnp.bfloat16)
    local_sums = jnp.einsum("htc,the->che", onehot, key_heads, preferred_element_type=jnp.float32)
    local_counts = jnp.swapaxes(jnp.sum(onehot, axis=1, dtype=jnp.float32), 0, 1)
    prior_weight = float(tok_rows * lax.axis_size("seq") // clusters)
    old_turned = jnp.swapaxes(old_centroids, 0, 1)
    share_rows = clusters // lax.axis_size("seq")
    first_row = lax.axis_index("seq") * share_rows
    total_sums, total_counts = lax.psum((local_sums, local_counts), "seq")
    updated = (total_sums + prior_weight * old_turned) / (total_counts[:, :, None] + prior_weight)
    centroid_low = updated.astype(jnp.bfloat16)
    own_rows = lax.dynamic_slice_in_dim(updated, first_row, share_rows, 0)
    new_centroids = jnp.swapaxes(own_rows, 0, 1)
    centroid_wide = centroid_low.astype(jnp.float32)
    centroid_square = jnp.swapaxes(jnp.sum(centroid_wide * centroid_wide, axis=2), 0, 1)
    key_wide = key_heads.astype(jnp.float32)
    key_square = jnp.swapaxes(jnp.sum(key_wide * key_wide, axis=2), 0, 1)
    cross_term = jnp.einsum(
        "the,che->htc", key_heads, centroid_low, preferred_element_type=jnp.float32
    )
    dist = (key_square[:, :, None] - 2.0 * cross_term + centroid_square[:, None, :]) / head_size
    return (key_cache, value_cache, new_centroids, dist.astype(jnp.bfloat16))


def solution(mesh):
    in_specs = (
        P("seq", "head"),
        P("head", "seq"),
        P("head", "seq"),
        P("head", "seq"),
        P("head", None, None),
    )
    out_specs = (P("seq", "head"), P("seq", "head"), P("head", "seq", None), P("head", "seq", None))
    return jax.shard_map(shards, mesh=mesh, in_specs=in_specs, out_specs=out_specs, check_vma=False)
```

profile of v0, /device:TPU:2, one launch (start us, length us, event | category | flops | bytes accessed | tf_op | source)
XLA Modules:
  0.0 438.8 jit_solution(4969922273733050903)
XLA Ops:
  7.2 0.0 copy-start
  7.2 0.0 all-gather.2.cloned.1.call-start
  7.2 1.5 pad_maximum_fusion
  8.7 0.0 all-gather.2.cloned.1.call-update
  8.8 0.0 reduce-scatter.2.cloned.1.call-start
  8.8 90.7 %all-gather.2.cloned.1.call-done = bf16[1024,2,1024]{0,2,1:T(8,128)(2,1)} async-done(((bf16[1024,2,16]{0,2,1:T(8,128)(2,1)}), bf16[1024,2,1024]{0,2,1:T(8,128)(2,1)}) %all-gather.2.cloned.1.call-update) | async-done | bytes 4194320 | tf_op jit(solution)/shard_map/all_gather | solution.py:16
  99.5 0.0 copy-done
  99.6 7.4 %convert_bitcast_fusion = bf16[768,2,1024]{0,2,1:T(8,128)(2,1)} fusion(bf16[1024,2,1024]{0,2,1:T(8,128)(2,1)} %all-gather.2.cloned.1.call-done, bf16[768,1024]{1,0:T(8,128)(2,1)S(1)} %copy-done), kind=kOutput, calls=%fused_computation.4 | convolution fusion | flops 3222798336 | bytes 8912896 | tf_op jit(solution)/shard_map/td,dkc->tkc/dot_general | solution.py:13
  106.9 0.0 copy-start.2
  106.9 0.0 copy-start.3
  106.9 0.0 reduce-scatter.2.cloned.1.call-update
  106.9 0.0 all-reduce.2.cloned.1.call-start
  107.0 1.0 copy-done.2
  108.0 0.2 copy.16
  108.2 0.0 copy-done.3
  108.2 0.4 convert_reduce_fusion
  108.6 122.6 %psum.15 = f32[1024,1]{0,1:T(1,128)S(1)} all-reduce(f32[1024,1]{0,1:T(1,128)S(1)} %bitcast.40), channel_id=1, replica_groups=mesh['seq'=64,'head'=8] {'seq'}, use_global_device_ids=true, to_apply=%region_3.0 | all-reduce | flops 1024 | bytes 8192 | tf_op jit(solution)/shard_map/psum | solution.py:34
  231.2 0.0 reduce-scatter.2.cloned.1.call-done
  231.3 0.0 copy-start.1
  231.3 2.6 fusion.7
  233.9 0.0 all-reduce.2.cloned.1.call-update
  233.9 1.0 slice_bitcast_fusion
  235.0 0.8 copy.18
  235.8 0.8 copy.19
  236.6 0.0 copy-done.1
  236.6 0.1 multiply_reduce_fusion.1
  236.6 191.9 %all-reduce.2.cloned.1.call-done = f32[1024,1,128]{0,2,1:T(8,128)} async-done(((f32[1024,1,128]{0,2,1:T(8,128)}), f32[1024,1,128]{0,2,1:T(8,128)}) %all-reduce.2.cloned.1.call-update) | async-done | bytes 524304 | tf_op jit(solution)/shard_map/psum | solution.py:34
  428.5 1.2 multiply_reduce_fusion
  429.7 0.1 constant_dynamic-slice_fusion
  429.8 0.7 copy.17
  430.4 1.8 fusion.6
  (2 shorter events, 0.0 us)
Async XLA Ops:
  7.2 92.4 %copy-start = (bf16[768,1024]{1,0:T(8,128)(2,1)S(1)}, bf16[768,1024]{1,0:T(8,128)(2,1)}, u32[]{:S(2)}) copy-start(bf16[768,1024]{1,0:T(8,128)(2,1)} %param.5) | copy-start | bytes 4718596
  7.2 92.4 %all-gather.2.cloned.1.call-start = ((), (), s32[]{:S(2)}) async-start(), calls=%async_computation.1 | async-start | bytes 4259840 | tf_op jit(solution)/shard_map/all_gather | solution.py:16
  8.8 222.5 %reduce-scatter.2.cloned.1.call-start = ((), (), s32[]{:S(2)}) async-start(), calls=%async_computation.2 | async-start | bytes 3538944 | tf_op jit(solution)/shard_map/reduce_scatter | solution.py:19
  106.9 1.0 copy-start.2
  106.9 1.2 copy-start.3
  106.9 321.6 %all-reduce.2.cloned.1.call-start = ((), (), s32[]{:S(2)}) async-start(), calls=%async_computation.3 | async-start | bytes 1048576 | tf_op jit(solution)/shard_map/psum | solution.py:34
  231.3 5.3 %copy-start.1 = (bf16[768,2,128]{0,2,1:T(8,128)(2,1)S(1)}, bf16[768,2,128]{0,2,1:T(8,128)(2,1)}, u32[]{:S(2)}) copy-start(bf16[768,2,128]{0,2,1:T(8,128)(2,1)} %reduce-scatter.2.cloned.1.call-done) | copy-start | bytes 1179652
Sparse Core Ops, SparseCore 0:
  12.0 87.5 all-gather.1
  107.1 49.0 reduce-scatter.1
  234.0 194.4 all-reduce.1
where the time goes:
time: 439 us
  waiting for transfers between devices  283 us (64%)
  blocking collectives  123 us (28%)
  between operations  13.8 us (3%)
  matrix products  11.8 us (3%)
  local copies, waits for them, and re-layouts  4.61 us (1%)
    psum x1, waiting for transfers between devices, shards(): total_sums, total_counts = lax.psum((local_sums, local_counts), 'seq')  192 us
    psum x1, blocking collectives, shards(): total_sums, total_counts = lax.psum((local_sums, local_counts), 'seq')  123 us
    all_gather x1, waiting for transfers between devices, shards(): lax.all_gather(stacked, 'seq', axis=2, tiled=True)  90.7 us
  transfers between devices with their start and end apart: 3, of which 2 were waited for; matrix products, arithmetic and copies ran while one was open for 1% of the time, Pallas kernels for 0%

commit v1 on v0

--- a/solution.py
+++ b/solution.py
@@ -2,6 +2,11 @@
 import jax.numpy as jnp
 from jax import lax
 from jax.sharding import PartitionSpec as P
+
+
+def _prepare_records(work_x, mesh_name):
+    reached = jnp.concatenate([work_x for _ in range(lax.psum(1, axis_name=mesh_name))], axis=2)
+    return lax.all_to_all(reached, concat_axis=2, tiled=True, split_axis=2, axis_name=mesh_name)
 
 
 def shards(hidden_states, k_weight, v_weight, assignments, old_centroids):
@@ -13,7 +18,7 @@
     partial_terms = jnp.einsum(
         "td,dkc->tkc",
         hidden_states,
-        lax.all_gather(stacked, "seq", axis=2, tiled=True),
+        _prepare_records(stacked, "seq"),
         preferred_element_type=jnp.float32,
     )
     summed = lax.psum_scatter(

time: 439 us -> 524 us (1.19)
  blocking collectives: 123 us -> 226 us
  waiting for transfers between devices: 283 us -> 194 us
  other arithmetic: 3.13 us -> 67.2 us
  local copies, waits for them, and re-layouts: 4.61 us -> 10.6 us
    all_to_all x0 -> x1, blocking collectives: none -> 107 us  [_prepare_records(): lax.all_to_all(reached, concat_axis=2, tiled=True, split_axis=2, axis_nam...]
    all_gather x1 -> x0, waiting for transfers between devices: 90.7 us -> none  [shards(): lax.all_gather(stacked, 'seq', axis=2, tiled=True)]
    unnamed x1 -> x64, other arithmetic: 0.02 us -> 64.1 us
    concatenate x0 -> x1, local copies, waits for them, and re-layouts: none -> 6.5 us  [_prepare_records(): jnp.concatenate([work_x for _ in range(lax.psum(1, axis_name=mesh_name))]...]
  transfers between devices with their start and end apart: 3 -> 2, of which waited for: 2 -> 1; matrix products, arithmetic and copies ran while one was open for 1% -> 1% of each run, Pallas kernels for 0% -> 0%
where the time goes in v1:
time: 524 us; the launch traced here: 522 us
  blocking collectives  226 us (43%)
  waiting for transfers between devices  194 us (37%)
  other arithmetic  67.2 us (13%)
  between operations  14.2 us (3%)
  local copies, waits for them, and re-layouts  10.6 us (2%)
  matrix products  9.48 us (2%)
    psum x1, waiting for transfers between devices, shards(): total_sums, total_counts = lax.psum((local_sums, local_counts), 'seq')  194 us
    psum x1, blocking collectives, shards(): total_sums, total_counts = lax.psum((local_sums, local_counts), 'seq')  119 us
    all_to_all x1, blocking collectives, _prepare_records(): lax.all_to_all(reached, concat_axis=2, tiled=True, split_axis=2, axis_nam...  107 us
    unnamed x64, other arithmetic  64.1 us
  transfers between devices with their start and end apart: 2, of which 1 were waited for; matrix products, arithmetic and copies ran while one was open for 1% of the time, Pallas kernels for 0%

profile of v1, /device:TPU:2, one launch (start us, length us, event | category | flops | bytes accessed | tf_op | source)
XLA Modules:
  0.0 521.7 jit_solution(4760827787588277690)
XLA Ops:
  7.2 1.5 constant_dynamic-update-slice_fusion.63
  8.7 1.4 constant_dynamic-update-slice_fusion.62
  10.1 1.4 constant_dynamic-update-slice_fusion.61
  11.5 1.4 constant_dynamic-update-slice_fusion.60
  12.9 1.4 constant_dynamic-update-slice_fusion.59
  14.3 1.4 constant_dynamic-update-slice_fusion.58
  15.7 1.4 constant_dynamic-update-slice_fusion.57
  17.1 1.4 constant_dynamic-update-slice_fusion.56
  18.5 1.4 constant_dynamic-update-slice_fusion.55
  19.9 1.4 constant_dynamic-update-slice_fusion.54
  21.3 1.4 constant_dynamic-update-slice_fusion.53
  22.7 1.4 constant_dynamic-update-slice_fusion.52
  24.1 1.4 constant_dynamic-update-slice_fusion.51
  25.5 1.4 constant_dynamic-update-slice_fusion.50
  26.9 1.4 constant_dynamic-update-slice_fusion.49
  28.3 1.4 constant_dynamic-update-slice_fusion.48
  29.7 1.4 constant_dynamic-update-slice_fusion.47
  31.1 1.4 constant_dynamic-update-slice_fusion.46
  32.5 1.4 constant_dynamic-update-slice_fusion.45
  33.9 1.4 constant_dynamic-update-slice_fusion.44
  35.3 1.4 constant_dynamic-update-slice_fusion.43
  36.7 1.4 constant_dynamic-update-slice_fusion.42
  38.1 1.4 constant_dynamic-update-slice_fusion.41
  39.5 1.4 constant_dynamic-update-slice_fusion.40
  40.9 1.4 constant_dynamic-update-slice_fusion.39
  42.3 1.4 constant_dynamic-update-slice_fusion.38
  43.7 1.4 constant_dynamic-update-slice_fusion.37
  45.1 1.4 constant_dynamic-update-slice_fusion.36
  46.5 1.4 constant_dynamic-update-slice_fusion.35
  47.9 1.4 constant_dynamic-update-slice_fusion.34
  49.3 1.4 constant_dynamic-update-slice_fusion.33
  50.7 1.4 constant_dynamic-update-slice_fusion.32
  52.1 0.6 constant_dynamic-update-slice_fusion.31
  52.7 0.6 constant_dynamic-update-slice_fusion.30
  53.3 0.6 constant_dynamic-update-slice_fusion.29
  53.9 0.6 constant_dynamic-update-slice_fusion.28
  55.2 0.6 constant_dynamic-update-slice_fusion.26
  56.4 0.6 constant_dynamic-update-slice_fusion.24
  57.7 0.6 constant_dynamic-update-slice_fusion.22
  60.2 0.6 constant_dynamic-update-slice_fusion.18
  60.8 0.6 constant_dynamic-update-slice_fusion.17
  61.4 0.6 constant_dynamic-update-slice_fusion.16
  63.9 0.6 constant_dynamic-update-slice_fusion.12
  65.1 0.6 constant_dynamic-update-slice_fusion.10
  66.4 0.6 constant_dynamic-update-slice_fusion.8
  67.6 0.6 constant_dynamic-update-slice_fusion.6
  68.3 0.6 constant_dynamic-update-slice_fusion.5
  69.5 0.6 constant_dynamic-update-slice_fusion.3
  70.1 0.6 constant_dynamic-update-slice_fusion.2
  70.7 0.6 constant_dynamic-update-slice_fusion.1
  71.4 0.6 constant_dynamic-update-slice_fusion
  72.0 6.5 %copy.27 = bf16[1024,2,1024]{0,1,2:T(2,128)(2,1)S(1)} copy(bf16[1024,2,1024]{0,2,1:T(8,128)(2,1)} %constant_dynamic-update-slice_fusion) | data formatting | bytes 8388608 | tf_op jit(solution)/shard_map/concatenate | solution.py:8
  78.5 106.7 %all_to_all.5 = bf16[1024,2,1024]{0,1,2:T(2,128)(2,1)S(1)} all-to-all(bf16[1024,2,1024]{0,1,2:T(2,128)(2,1)S(1)} %copy.27), channel_id=1, replica_groups=mesh['seq'=64,'head'=8] {'seq'}, dimensions={2} | all-to-all | bytes 8388608 | tf_op jit(solution)/shard_map/all_to_all | solution.py:9
  185.2 5.1 convert_bitcast_fusion
  191.3 119.0 %psum.15 = f32[1024,1]{0,1:T(1,128)S(1)} all-reduce(f32[1024,1]{0,1:T(1,128)S(1)} %bitcast.165), channel_id=1, replica_groups=mesh['seq'=64,'head'=8] {'seq'}, use_global_device_ids=true, to_apply=%region_3.0 | all-reduce | flops 1024 | bytes 8192 | tf_op jit(solution)/shard_map/psum | solution.py:39
  310.4 2.6 fusion.11
  313.0 1.0 slice_bitcast_fusion
  314.1 0.8 copy.31
  314.9 0.8 copy.32
  315.7 1.0 multiply_reduce_fusion.1
  316.7 194.4 %all-reduce.2.cloned.1.call-done = f32[1024,1,128]{0,2,1:T(8,128)} async-done(((f32[1024,1,128]{0,2,1:T(8,128)}), f32[1024,1,128]{0,2,1:T(8,128)}) %all-reduce.2.cloned.1.call-update) | async-done | bytes 524304 | tf_op jit(solution)/shard_map/psum | solution.py:39
  511.1 1.2 multiply_reduce_fusion
  512.3 0.7 copy.30
  513.0 1.8 fusion.10
  (35 shorter events, 9.3 us)
Async XLA Ops:
  7.2 178.0 %copy-start = (bf16[768,1024]{1,0:T(8,128)(2,1)S(1)}, bf16[768,1024]{1,0:T(8,128)(2,1)}, u32[]{:S(2)}) copy-start(bf16[768,1024]{1,0:T(8,128)(2,1)} %param.5) | copy-start | bytes 4718596
  7.2 44.9 %copy-start.2 = (bf16[1024,16]{0,1:T(8,128)(2,1)S(1)}, bf16[1024,16]{0,1:T(8,128)(2,1)}, u32[]{:S(2)}) copy-start(bf16[1024,16]{0,1:T(8,128)(2,1)} %param.6) | copy-start | bytes 98308
  7.2 44.9 %copy-start.1 = (bf16[1024,16]{0,1:T(8,128)(2,1)S(1)}, bf16[1024,16]{0,1:T(8,128)(2,1)}, u32[]{:S(2)}) copy-start(bf16[1024,16]{0,1:T(8,128)(2,1)} %param.7) | copy-start | bytes 98308
  7.2 303.1 %reduce-scatter.2.cloned.1.call-start = ((), (), s32[]{:S(2)}) async-start(), calls=%async_computation.2 | async-start | bytes 3538944 | tf_op jit(solution)/shard_map/reduce_scatter | solution.py:24
  185.2 5.1 copy-start.4
  190.2 0.7 copy-start.5
  190.2 320.8 %all-reduce.2.cloned.1.call-start = ((), (), s32[]{:S(2)}) async-start(), calls=%async_computation.3 | async-start | bytes 1048576 | tf_op jit(solution)/shard_map/psum | solution.py:39
  310.4 202.7 %copy-start.3 = (bf16[768,2,128]{0,2,1:T(8,128)(2,1)S(1)}, bf16[768,2,128]{0,2,1:T(8,128)(2,1)}, u32[]{:S(2)}) copy-start(bf16[768,2,128]{0,2,1:T(8,128)(2,1)} %reduce-scatter.2.cloned.1.call-done) | copy-start | bytes 1179652
Sparse Core Ops, SparseCore 0:
  190.4 49.4 reduce-scatter.1
  313.1 197.9 all-reduce.1
